TPU v7x, 256 devices: a whole 4x4x8 slice. The times are simulated.
256 devices in a mesh: row: 64 (over z, x, core), col: 4 (over y).
Axes of the slice: x: 4, y: 4, z: 8, core: 2. Of those that a mesh axis runs over, the one named last changes fastest.
Arguments:
- eigen_vectors: float32 [65536, 2048], P('row', 'col'), may hold values from -6 to 6
- panel_first: float32 [65536, 512], P('row', 'col'), may hold values from -0.0234375 to 0.0234375
- panel_second: float32 [65536, 512], P('row', 'col'), may hold values from -0.0234375 to 0.0234375
- factor_first: float32 [512, 512], replicated, as said below
- factor_second: float32 [512, 512], replicated, as said below
Outputs:
- transformed: float32 [65536, 2048], P('row', 'col')
Inputs may be any that keep to these rules, and one draw needn't show every extreme that they name: factor_first is upper triangular. factor_second is upper triangular.
All inputs are finite; a program needn't handle non-finite values.
Results may differ from a plain program's by a relative error of at most 0.0001.
Values sent between devices are 32-bit elements; how exact they have to be, the bound alone decides.
A program may use at most 64 MiB of HBM per device.

v0:
```python
import jax
import jax.numpy as jnp
from jax import lax
from jax.sharding import PartitionSpec as P


def local_dot(left, right):
    return jnp.dot(left, right, precision=lax.Precision.HIGHEST, preferred_element_type=jnp.float32)


def on_device(eigen_vectors, panel_first, panel_second, factor_first, factor_second):
    vectors_first, vectors_second = (
        lax.all_gather(panel_first, "col", axis=1, tiled=True),
        lax.all_gather(panel_second, "col", axis=1, tiled=True),
    )
    updated = eigen_vectors
    for vectors, factor in ((vectors_second, factor_second), (vectors_first, factor_first)):
        projected = lax.psum(local_dot(vectors.T, updated), "row")
        updated = updated - local_dot(vectors, local_dot(factor, projected))
    return updated


def solution(mesh):
    return jax.shard_map(
        on_device,
        mesh=mesh,
        in_specs=(P("row", "col"), P("row", "col"), P("row", "col"), P(), P()),
        out_specs=P("row", "col"),
        check_vma=False,
    )
```

profile of v0, /device:TPU:2, one launch (start us, length us, event | category | flops | bytes accessed | tf_op | source)
XLA Modules:
  0.0 489.9 jit_solution(13519576373823585658)
XLA Ops:
  6.5 0.0 copy-start
  6.5 0.0 all-gather.3.cloned.1.call-start
  6.5 0.7 all-gather.3.cloned.1.call-update
  7.3 0.0 all-reduce.3.cloned.1.call-start
  7.3 41.9 %all-gather.3.cloned.1.call-done = f32[1024,512]{1,0:T(8,128)} async-done(((f32[1024,128]{1,0:T(8,128)}), f32[1024,512]{1,0:T(8,128)}) %all-gather.3.cloned.1.call-update) | async-done | bytes 2097168 | tf_op jit(solution)/shard_map/all_gather | solution.py:14
  49.2 0.0 copy-start.3
  49.2 6.9 %fusion = f32[512,512]{1,0:T(8,128)} fusion(f32[1024,512]{1,0:T(8,128)} %all-gather.3.cloned.1.call-done, f32[1024,512]{1,0:T(8,128)} %param.5), kind=kOutput, calls=%fused_computation.3 | convolution fusion | flops 3221225472 | bytes 5242880 | tf_op jit(solution)/shard_map/dot_general | solution.py:8
  56.1 0.0 all-reduce.3.cloned.1.call-update
  56.1 0.0 all-gather.5.cloned.1.call-start
  56.1 0.7 all-gather.5.cloned.1.call-update
  56.8 0.0 all-reduce.5.cloned.1.call-start
  56.9 0.0 copy-done.3
  56.9 1.8 copy.6
  58.7 183.9 %all-reduce.3.cloned.1.call-done = f32[512,512]{1,0:T(8,128)} async-done(((f32[512,512]{1,0:T(8,128)}), f32[512,512]{1,0:T(8,128)}) %all-reduce.3.cloned.1.call-update) | async-done | bytes 1048592 | tf_op jit(solution)/shard_map/psum | solution.py:18
  242.6 0.0 copy-done
  242.6 0.0 copy-start.1
  242.6 4.8 fusion.1
  247.4 0.0 copy-done.1
  247.5 5.2 %bitcast_subtract_fusion.1 = f32[1024,512]{0,1:T(8,128)S(1)} fusion(f32[1024,512]{0,1:T(8,128)} %copy.6, f32[512,512]{1,0:T(8,128)S(1)} %fusion.1, f32[1024,512]{1,0:T(8,128)S(1)} %copy-done.1), kind=kOutput, calls=%fused_computation.1 | convolution fusion | flops 3221749760 | bytes 7340032 | tf_op jit(solution)/shard_map/dot_general | solution.py:8
  252.6 26.6 %all-gather.5.cloned.1.call-done = f32[1024,512]{1,0:T(8,128)} async-done(((f32[1024,128]{1,0:T(8,128)}), f32[1024,512]{1,0:T(8,128)}) %all-gather.5.cloned.1.call-update) | async-done | bytes 2097168 | tf_op jit(solution)/shard_map/all_gather | solution.py:13
  279.2 6.1 %convolution_bitcast_fusion = f32[512,512]{0,1:T(8,128)} fusion(f32[1024,512]{0,1:T(8,128)S(1)} %bitcast_subtract_fusion.1, f32[1024,512]{1,0:T(8,128)} %all-gather.5.cloned.1.call-done), kind=kOutput, calls=%fused_computation.2 | convolution fusion | flops 3221225472 | bytes 5242880 | tf_op jit(solution)/shard_map/dot_general | solution.py:8
  285.3 0.0 all-reduce.5.cloned.1.call-update
  285.3 186.5 %all-reduce.5.cloned.1.call-done = f32[512,512]{0,1:T(8,128)} async-done(((f32[512,512]{0,1:T(8,128)}), f32[512,512]{0,1:T(8,128)}) %all-reduce.5.cloned.1.call-update) | async-done | bytes 1048592 | tf_op jit(solution)/shard_map/psum | solution.py:18
  471.8 0.0 copy-start.2
  471.8 3.5 fusion.2
  475.4 0.0 copy-done.2
  475.4 5.1 %bitcast_subtract_fusion = f32[1024,512]{0,1:T(8,128)} fusion(f32[1024,512]{0,1:T(8,128)S(1)} %bitcast_subtract_fusion.1, f32[512,512]{1,0:T(8,128)S(1)} %fusion.2, f32[1024,512]{1,0:T(8,128)S(1)} %copy-done.2), kind=kOutput, calls=%fused_computation | convolution fusion | flops 3221749760 | bytes 7340032 | tf_op jit(solution)/shard_map/dot_general | solution.py:8
  480.5 2.9 copy.7
Async XLA Ops:
  6.5 236.1 %copy-start = (f32[512,512]{1,0:T(8,128)S(1)}, f32[512,512]{1,0:T(8,128)}, u32[]{:S(2)}) copy-start(f32[512,512]{1,0:T(8,128)} %param.9) | copy-start | bytes 3145732
  6.5 42.7 %all-gather.3.cloned.1.call-start = ((), (), s32[]{:S(2)}) async-start(), calls=%async_computation | async-start | bytes 2621440 | tf_op jit(solution)/shard_map/all_gather | solution.py:14
  7.3 235.3 %all-reduce.3.cloned.1.call-start = ((), (), s32[]{:S(2)}) async-start(), calls=%async_computation.1 | async-start | bytes 2097152 | tf_op jit(solution)/shard_map/psum | solution.py:18
  49.2 7.7 %copy-start.3 = (f32[1024,512]{1,0:T(8,128)S(1)}, f32[1024,512]{1,0:T(8,128)}, u32[]{:S(2)}) copy-start(f32[1024,512]{1,0:T(8,128)} %param.5) | copy-start | bytes 6291460
  56.1 223.1 %all-gather.5.cloned.1.call-start = ((), (), s32[]{:S(2)}) async-start(), calls=%async_computation.2 | async-start | bytes 2621440 | tf_op jit(solution)/shard_map/all_gather | solution.py:13
  56.8 415.0 %all-reduce.5.cloned.1.call-start = ((), (), s32[]{:S(2)}) async-start(), calls=%async_computation.3 | async-start | bytes 2097152 | tf_op jit(solution)/shard_map/psum | solution.py:18
  242.6 4.9 copy-start.1
  471.8 3.6 copy-start.2
Sparse Core Ops, SparseCore 0:
  9.2 40.0 all-gather.2
  56.2 186.3 all-reduce.2
  244.5 34.6 all-gather.4
  285.4 186.3 all-reduce.4
where the time goes:
time: 490 us
  waiting for transfers between devices  440 us (90%)
  matrix products  31.6 us (6%)
  between operations  13.2 us (3%)
    psum x2, waiting for transfers between devices, on_device(): projected = lax.psum(local_dot(vectors.T, updated), 'row')  370 us
    all_gather x1, waiting for transfers between devices, on_device(): lax.all_gather(panel_second, 'col', axis=1, tiled=True)  41.9 us
    dot_general x6, matrix products, local_dot(): jnp.dot(left, right, precision=lax.Precision.HIGHEST, preferred_element_t...  31.6 us
    all_gather x1, waiting for transfers between devices, on_device(): lax.all_gather(panel_first, 'col', axis=1, tiled=True)  26.6 us
  transfers between devices with their start and end apart: 4, of which 4 were waited for; matrix products, arithmetic and copies ran while one was open for 2% of the time, Pallas kernels for 0%

commit v1 on v0

--- a/solution.py
+++ b/solution.py
@@ -2,6 +2,11 @@
 import jax.numpy as jnp
 from jax import lax
 from jax.sharding import PartitionSpec as P
+
+
+def exchange_gather(x, mesh_axis, dim):
+    stack = jnp.stack([x] * lax.axis_size(mesh_axis))
+    return jnp.concatenate(lax.all_to_all(stack, mesh_axis, 0, 0), axis=dim)
 
 
 def local_dot(left, right):
@@ -10,7 +15,7 @@
 
 def on_device(eigen_vectors, panel_first, panel_second, factor_first, factor_second):
     vectors_first, vectors_second = (
-        lax.all_gather(panel_first, "col", axis=1, tiled=True),
+        exchange_gather(panel_first, "col", 1),
         lax.all_gather(panel_second, "col", axis=1, tiled=True),
     )
     updated = eigen_vectors

time: 490 us -> 474 us (0.967)
  waiting for transfers between devices: 440 us -> 416 us
    all_gather x1 -> x0, waiting for transfers between devices: 26.6 us -> none  [on_device(): lax.all_gather(panel_first, 'col', axis=1, tiled=True)]
    all_gather x1, waiting for transfers between devices: 41.9 us -> 47.2 us  [on_device(): lax.all_gather(panel_second, 'col', axis=1, tiled=True)]
  transfers between devices with their start and end apart: 4 -> 4, of which waited for: 4 -> 3; matrix products, arithmetic and copies ran while one was open for 2% -> 4% of each run, Pallas kernels for 0% -> 0%
where the time goes in v1:
time: 474 us; the launch traced here: 473 us
  waiting for transfers between devices  416 us (88%)
  matrix products  32.3 us (7%)
  between operations  13.2 us (3%)
  local copies, waits for them, and re-layouts  7.54 us (2%)
    psum x2, waiting for transfers between devices, on_device(): projected = lax.psum(local_dot(vectors.T, updated), 'row')  368 us
    all_gather x1, waiting for transfers between devices, on_device(): lax.all_gather(panel_second, 'col', axis=1, tiled=True)  47.2 us
    dot_general x6, matrix products, local_dot(): jnp.dot(left, right, precision=lax.Precision.HIGHEST, preferred_element_t...  32.3 us
  transfers between devices with their start and end apart: 4, of which 3 were waited for; matrix products, arithmetic and copies ran while one was open for 4% of the time, Pallas kernels for 0%

profile of v1, /device:TPU:2, one launch (start us, length us, event | category | flops | bytes accessed | tf_op | source)
XLA Modules:
  0.0 473.4 jit_solution(1854935202438279240)
XLA Ops:
  6.5 0.0 copy-start
  6.5 0.0 all-gather.2.cloned.1.call-start
  6.5 0.7 all-gather.2.cloned.1.call-update
  7.3 1.2 copy.9
  8.5 1.6 stack.2
  10.1 0.0 copy-start.2
  10.1 4.6 all-to-all-start
  14.7 0.0 all-reduce.3.cloned.1.call-start
  14.7 47.2 %all-gather.2.cloned.1.call-done = f32[1024,512]{1,0:T(8,128)} async-done(((f32[1024,128]{1,0:T(8,128)}), f32[1024,512]{1,0:T(8,128)}) %all-gather.2.cloned.1.call-update) | async-done | bytes 2097168 | tf_op jit(solution)/shard_map/all_gather | solution.py:19
  61.9 0.0 copy-done.2
  61.9 6.1 %fusion = f32[512,512]{1,0:T(8,128)} fusion(f32[1024,512]{1,0:T(8,128)} %all-gather.2.cloned.1.call-done, f32[1024,512]{1,0:T(8,128)S(1)} %copy-done.2), kind=kOutput, calls=%fused_computation.3 | convolution fusion | flops 3221225472 | bytes 5242880 | tf_op jit(solution)/shard_map/dot_general | solution.py:13
  68.0 0.0 all-reduce.3.cloned.1.call-update
  68.0 0.0 all-reduce.5.cloned.1.call-start
  68.1 1.8 copy.8
  69.9 184.7 %all-reduce.3.cloned.1.call-done = f32[512,512]{1,0:T(8,128)} async-done(((f32[512,512]{1,0:T(8,128)}), f32[512,512]{1,0:T(8,128)}) %all-reduce.3.cloned.1.call-update) | async-done | bytes 1048592 | tf_op jit(solution)/shard_map/psum | solution.py:23
  254.6 0.0 copy-done
  254.6 0.0 copy-start.1
  254.6 4.8 %fusion.1 = f32[512,512]{1,0:T(8,128)S(1)} fusion(f32[512,512]{1,0:T(8,128)} %all-reduce.3.cloned.1.call-done, f32[512,512]{1,0:T(8,128)S(1)} %copy-done), kind=kOutput, calls=%fused_computation.4 | convolution fusion | flops 1610612736 | bytes 3145728 | tf_op jit(solution)/shard_map/dot_general | solution.py:13
  259.5 0.0 copy-done.1
  259.5 5.2 %bitcast_subtract_fusion.1 = f32[1024,512]{0,1:T(8,128)S(1)} fusion(f32[1024,512]{0,1:T(8,128)} %copy.8, f32[512,512]{1,0:T(8,128)S(1)} %fusion.1, f32[1024,512]{1,0:T(8,128)S(1)} %copy-done.1), kind=kOutput, calls=%fused_computation.1 | convolution fusion | flops 3221749760 | bytes 7340032 | tf_op jit(solution)/shard_map/dot_general | solution.py:13
  264.7 0.0 all-to-all-done
  264.7 6.1 %convolution_bitcast_fusion = f32[512,512]{0,1:T(8,128)} fusion(f32[1024,512]{0,1:T(8,128)S(1)} %bitcast_subtract_fusion.1, f32[1024,512]{0,1:T(8,128)} %bitcast.2), kind=kOutput, calls=%fused_computation.2 | convolution fusion | flops 3221225472 | bytes 5242880 | tf_op jit(solution)/shard_map/dot_general | solution.py:13
  270.7 0.0 all-reduce.5.cloned.1.call-update
  270.8 183.1 %all-reduce.5.cloned.1.call-done = f32[512,512]{0,1:T(8,128)} async-done(((f32[512,512]{0,1:T(8,128)}), f32[512,512]{0,1:T(8,128)}) %all-reduce.5.cloned.1.call-update) | async-done | bytes 1048592 | tf_op jit(solution)/shard_map/psum | solution.py:23
  453.9 3.6 fusion.2
  457.5 6.5 %bitcast_subtract_fusion = f32[1024,512]{0,1:T(8,128)} fusion(f32[1024,512]{0,1:T(8,128)S(1)} %bitcast_subtract_fusion.1, f32[512,512]{1,0:T(8,128)S(1)} %fusion.2, f32[1024,512]{0,1:T(8,128)} %bitcast.2), kind=kOutput, calls=%fused_computation | convolution fusion | flops 3221749760 | bytes 7340032 | tf_op jit(solution)/shard_map/dot_general | solution.py:13
  464.0 2.9 copy.10
Async XLA Ops:
  6.5 248.1 %copy-start = (f32[512,512]{1,0:T(8,128)S(1)}, f32[512,512]{1,0:T(8,128)}, u32[]{:S(2)}) copy-start(f32[512,512]{1,0:T(8,128)} %param.9) | copy-start | bytes 3145732
  6.5 55.4 %all-gather.2.cloned.1.call-start = ((), (), s32[]{:S(2)}) async-start(), calls=%async_computation.1 | async-start | bytes 2621440 | tf_op jit(solution)/shard_map/all_gather | solution.py:19
  10.1 51.8 %copy-start.2 = (f32[1024,512]{1,0:T(8,128)S(1)}, f32[1024,512]{1,0:T(8,128)}, u32[]{:S(2)}) copy-start(f32[1024,512]{1,0:T(8,128)} %param.5) | copy-start | bytes 6291460
  10.1 254.5 %all-to-all-start = ((f32[4,1024,128]{1,2,0:T(8,128)}), f32[4,1024,128]{1,2,0:T(8,128)}, u32[]{:S(2)}, u32[]{:S(2)}) async-start(f32[4,1024,128]{1,2,0:T(8,128)} %stack.2), calls=%async_computation | async-start | bytes 4194304 | tf_op jit(solution)/shard_map/all_to_all | solution.py:9
  14.7 239.9 %all-reduce.3.cloned.1.call-start = ((), (), s32[]{:S(2)}) async-start(), calls=%async_computation.2 | async-start | bytes 2097152 | tf_op jit(solution)/shard_map/psum | solution.py:23
  68.0 385.8 %all-reduce.5.cloned.1.call-start = ((), (), s32[]{:S(2)}) async-start(), calls=%async_computation.3 | async-start | bytes 2097152 | tf_op jit(solution)/shard_map/psum | solution.py:23
  254.6 4.9 %copy-start.1 = (f32[1024,512]{1,0:T(8,128)S(1)}, f32[1024,512]{1,0:T(8,128)}, u32[]{:S(2)}) copy-start(f32[1024,512]{1,0:T(8,128)} %all-gather.2.cloned.1.call-done) | copy-start | bytes 6291460
Sparse Core Ops, SparseCore 0:
  9.2 52.7 all-gather.1
  68.2 186.3 all-reduce.2
  270.9 182.9 all-reduce.4

commit v2 on v0

--- a/solution.py
+++ b/solution.py
@@ -2,6 +2,27 @@
 import jax.numpy as jnp
 from jax import lax
 from jax.sharding import PartitionSpec as P
+
+
+def collect(shard, axis, dim):
+    size, index, extent = (lax.axis_size(axis), lax.axis_index(axis), shard.shape[dim])
+    right = [(i, (i + 1) % size) for i in range(size)]
+    left = [(i, (i - 1) % size) for i in range(size)]
+    out = jnp.zeros((*shard.shape[:dim], size * extent, *shard.shape[dim + 1 :]), shard.dtype)
+    out = lax.dynamic_update_slice_in_dim(out, shard, index * extent, axis=dim)
+    from_left = from_right = shard
+    half = size // 2
+    for step in range(1, half + 1):
+        from_left = lax.ppermute(from_left, axis, right)
+        out = lax.dynamic_update_slice_in_dim(
+            out, from_left, (index - step) % size * extent, axis=dim
+        )
+        if step < size - half:
+            from_right = lax.ppermute(from_right, axis, left)
+            out = lax.dynamic_update_slice_in_dim(
+                out, from_right, (index + step) % size * extent, axis=dim
+            )
+    return out
 
 
 def local_dot(left, right):
@@ -11,7 +32,7 @@
 def on_device(eigen_vectors, panel_first, panel_second, factor_first, factor_second):
     vectors_first, vectors_second = (
         lax.all_gather(panel_first, "col", axis=1, tiled=True),
-        lax.all_gather(panel_second, "col", axis=1, tiled=True),
+        collect(panel_second, "col", 1),
     )
     updated = eigen_vectors
     for vectors, factor in ((vectors_second, factor_second), (vectors_first, factor_first)):

time: 490 us -> 445 us (0.908)
  waiting for transfers between devices: 440 us -> 395 us
    all_gather x1 -> x0, waiting for transfers between devices: 41.9 us -> none  [on_device(): lax.all_gather(panel_second, 'col', axis=1, tiled=True)]
    all_gather x1, waiting for transfers between devices: 26.6 us -> 0.03 us  [on_device(): lax.all_gather(panel_first, 'col', axis=1, tiled=True)]
    ppermute x0 -> x3, waiting for transfers between devices: none -> 25.3 us  [the longest x2 25.2 us: collect(): from_left = lax.ppermute(from_left, axis, right)]
  transfers between devices with their start and end apart: 4 -> 6, of which waited for: 4 -> 4; matrix products, arithmetic and copies ran while one was open for 2% -> 2% of each run, Pallas kernels for 0% -> 0%
where the time goes in v2:
time: 445 us
  waiting for transfers between devices  395 us (89%)
  matrix products  29.7 us (7%)
  between operations  15 us (3%)
    psum x2, waiting for transfers between devices, on_device(): projected = lax.psum(local_dot(vectors.T, updated), 'row')  369 us
    dot_general x6, matrix products, local_dot(): jnp.dot(left, right, precision=lax.Precision.HIGHEST, preferred_element_t...  29.7 us
    ppermute x2, waiting for transfers between devices, collect(): from_left = lax.ppermute(from_left, axis, right)  25.2 us
  transfers between devices with their start and end apart: 6, of which 4 were waited for; matrix products, arithmetic and copies ran while one was open for 2% of the time, Pallas kernels for 0%

profile of v2, /device:TPU:2, one launch (start us, length us, event | category | flops | bytes accessed | tf_op | source)
XLA Modules:
  0.0 445.1 jit_solution(15920913346903934602)
XLA Ops:
  7.4 0.0 copy-start
  7.4 0.0 all-reduce.3.cloned.1.call-start
  7.4 1.6 collective-permute-start
  9.0 1.7 collective-permute-start.1
  10.6 11.9 %collective-permute-done = f32[1024,128]{1,0:T(8,128)S(1)} collective-permute-done((f32[1024,128]{1,0:T(8,128)}, f32[1024,128]{1,0:T(8,128)S(1)}, u32[]{:S(2)}, u32[]{:S(2)}) %collective-permute-start) | collective-permute-done | bytes 524320 | tf_op jit(solution)/shard_map/ppermute | solution.py:16
  22.6 0.3 collective-permute-start.2
  22.8 0.2 broadcast_in_dim.3
  23.1 0.0 copy-done.4
  23.1 0.0 copy-start.2
  23.1 0.1 constant_dynamic-update-slice_fusion.3
  23.2 0.1 constant_dynamic-update-slice_fusion.2
  23.3 0.0 collective-permute-done.1
  23.3 0.1 constant_dynamic-update-slice_fusion.1
  23.3 13.3 %collective-permute-done.2 = f32[1024,128]{1,0:T(8,128)S(1)} collective-permute-done((f32[1024,128]{1,0:T(8,128)S(1)}, f32[1024,128]{1,0:T(8,128)S(1)}, u32[]{:S(2)}, u32[]{:S(2)}) %collective-permute-start.2) | collective-permute-done | bytes 524320 | tf_op jit(solution)/shard_map/ppermute | solution.py:16
  36.7 0.1 constant_dynamic-update-slice_fusion
  36.7 0.0 copy-start.1
  36.7 1.3 copy-done.1
  38.0 0.0 copy-done.2
  38.1 4.6 %fusion = f32[512,512]{1,0:T(8,128)} fusion(f32[1024,512]{1,0:T(8,128)S(1)} %constant_dynamic-update-slice_fusion, f32[1024,512]{1,0:T(8,128)S(1)} %copy-done.2), kind=kOutput, calls=%fused_computation.7 | convolution fusion | flops 3221225472 | bytes 5242880 | tf_op jit(solution)/shard_map/dot_general | solution.py:29
  42.7 0.0 all-reduce.3.cloned.1.call-update
  42.7 0.0 all-gather.2.cloned.1.call-start
  42.7 0.5 all-gather.2.cloned.1.call-update
  43.3 0.2 all-reduce.5.cloned.1.call-start
  43.5 186.0 %all-reduce.3.cloned.1.call-done = f32[512,512]{1,0:T(8,128)} async-done(((f32[512,512]{1,0:T(8,128)}), f32[512,512]{1,0:T(8,128)}) %all-reduce.3.cloned.1.call-update) | async-done | bytes 1048592 | tf_op jit(solution)/shard_map/psum | solution.py:39
  229.5 4.7 %fusion.1 = f32[512,512]{1,0:T(8,128)S(1)} fusion(f32[512,512]{1,0:T(8,128)} %all-reduce.3.cloned.1.call-done, f32[512,512]{1,0:T(8,128)S(1)} %copy-done), kind=kOutput, calls=%fused_computation.8 | convolution fusion | flops 1610612736 | bytes 3145728 | tf_op jit(solution)/shard_map/dot_general | solution.py:29
  234.2 5.7 %convolution_subtract_fusion = f32[1024,512]{1,0:T(8,128)S(1)} fusion(f32[1024,512]{1,0:T(8,128)} %param.5, f32[1024,512]{1,0:T(8,128)} %copy-done.1, f32[512,512]{1,0:T(8,128)S(1)} %fusion.1), kind=kOutput, calls=%fused_computation.1 | convolution fusion | flops 3221749760 | bytes 7340032 | tf_op jit(solution)/shard_map/dot_general | solution.py:29
  239.9 0.0 all-gather.2.cloned.1.call-done
  239.9 6.1 %convolution_bitcast_fusion = f32[512,512]{0,1:T(8,128)} fusion(f32[1024,512]{1,0:T(8,128)S(1)} %convolution_subtract_fusion, f32[1024,512]{1,0:T(8,128)} %all-gather.2.cloned.1.call-done), kind=kOutput, calls=%fused_computation.2 | convolution fusion | flops 3221225472 | bytes 5242880 | tf_op jit(solution)/shard_map/dot_general | solution.py:29
  245.9 0.0 all-reduce.5.cloned.1.call-update
  246.0 183.1 %all-reduce.5.cloned.1.call-done = f32[512,512]{0,1:T(8,128)} async-done(((f32[512,512]{0,1:T(8,128)}), f32[512,512]{0,1:T(8,128)}) %all-reduce.5.cloned.1.call-update) | async-done | bytes 1048592 | tf_op jit(solution)/shard_map/psum | solution.py:39
  429.0 3.8 fusion.2
  432.8 4.8 %bitcast_subtract_fusion = f32[1024,512]{1,0:T(8,128)} fusion(f32[1024,512]{1,0:T(8,128)S(1)} %convolution_subtract_fusion, f32[512,512]{1,0:T(8,128)S(1)} %fusion.2, f32[1024,512]{1,0:T(8,128)S(1)} %copy-done.3), kind=kOutput, calls=%fused_computation | convolution fusion | flops 3221749760 | bytes 7340032 | tf_op jit(solution)/shard_map/dot_general | solution.py:29
  (4 shorter events, 0.0 us)
Async XLA Ops:
  7.4 222.1 %copy-start = (f32[512,512]{1,0:T(8,128)S(1)}, f32[512,512]{1,0:T(8,128)}, u32[]{:S(2)}) copy-start(f32[512,512]{1,0:T(8,128)} %param.9) | copy-start | bytes 3145732
  7.4 15.7 %copy-start.4 = (f32[1024,128]{1,0:T(8,128)S(1)}, f32[1024,128]{1,0:T(8,128)}, u32[]{:S(2)}) copy-start(f32[1024,128]{1,0:T(8,128)} %param.7) | copy-start | bytes 1572868
  7.4 222.1 %all-reduce.3.cloned.1.call-start = ((), (), s32[]{:S(2)}) async-start(), calls=%async_computation | async-start | bytes 2097152 | tf_op jit(solution)/shard_map/psum | solution.py:39
  7.4 15.2 %collective-permute-start = (f32[1024,128]{1,0:T(8,128)}, f32[1024,128]{1,0:T(8,128)S(1)}, u32[]{:S(2)}, u32[]{:S(2)}) collective-permute-start(f32[1024,128]{1,0:T(8,128)} %param.7), channel_id=1, source_target_pairs={{0,1},{1,2},{2,3},{3,0},{4,5},{5,6},{6,7},{7,4},{8,9},{9,10},{10,1... | collective-permute-start | bytes 1572872 | tf_op jit(solution)/shard_map/ppermute | solution.py:16
  9.0 14.3 %collective-permute-start.1 = (f32[1024,128]{1,0:T(8,128)}, f32[1024,128]{1,0:T(8,128)S(1)}, u32[]{:S(2)}, u32[]{:S(2)}) collective-permute-start(f32[1024,128]{1,0:T(8,128)} %param.7), channel_id=1, source_target_pairs={{0,3},{1,0},{2,1},{3,2},{4,7},{5,4},{6,5},{7,6},{8,11},{9,8},{10,9... | collective-permute-start | bytes 1572872 | tf_op jit(solution)/shard_map/ppermute | solution.py:21
  22.6 14.1 %collective-permute-start.2 = (f32[1024,128]{1,0:T(8,128)S(1)}, f32[1024,128]{1,0:T(8,128)S(1)}, u32[]{:S(2)}, u32[]{:S(2)}) collective-permute-start(f32[1024,128]{1,0:T(8,128)S(1)} %collective-permute-done), channel_id=1, source_target_pairs={{0,1},{1,2},{2,3},{3,0},{4,5},{5,6},{6,7},{7,4},{8,9},{9,10},{10,1... | collective-permute-start | bytes 1572872 | tf_op jit(solution)/shard_map/ppermute | solution.py:16
  23.1 15.0 %copy-start.2 = (f32[1024,512]{1,0:T(8,128)S(1)}, f32[1024,512]{1,0:T(8,128)}, u32[]{:S(2)}) copy-start(f32[1024,512]{1,0:T(8,128)} %param.5) | copy-start | bytes 6291460
  36.7 1.3 copy-start.1
  42.7 197.2 %all-gather.2.cloned.1.call-start = ((), (), s32[]{:S(2)}) async-start(), calls=%async_computation.1 | async-start | bytes 2621440 | tf_op jit(solution)/shard_map/all_gather | solution.py:34
  43.3 385.8 %all-reduce.5.cloned.1.call-start = ((), (), s32[]{:S(2)}) async-start(), calls=%async_computation.2 | async-start | bytes 2097152 | tf_op jit(solution)/shard_map/psum | solution.py:39
  429.0 3.8 copy-start.3
Sparse Core Ops, SparseCore 0:
  42.8 186.5 all-reduce.2
  246.1 182.8 all-reduce.4
Sparse Core Ops, SparseCore 1:
  45.1 37.0 all-gather.1
